TPU v7x, 128 devices: a whole 4x4x4 slice. The times are simulated.
128 devices in a mesh: req: 16 (over y, x), tp: 8 (over z, core).
Axes of the slice: x: 4, y: 4, z: 4, core: 2. Of those that a mesh axis runs over, the one named last changes fastest.
Arguments:
- stream: bfloat16 [512, 2048], P('req'), may hold values from -1.5 to 1.5
- attn_gain: bfloat16 [2048], replicated, may hold values from 0.25 to 1.75
- mlp_gain: bfloat16 [2048], replicated, may hold values from 0.25 to 1.75
- w_query: bfloat16 [2048, 2048], P(None, 'tp'), may hold values from -0.125 to 0.125
- w_keyval: bfloat16 [2048, 2, 2048], P(None, None, 'tp'), may hold values from -30 to 30
- w_out: bfloat16 [2048, 2048], P('tp'), may hold values from -0.125 to 0.125
- w_gate_up: bfloat16 [2048, 2, 8192], P(None, None, 'tp'), may hold values from -0.125 to 0.125
- w_down: bfloat16 [8192, 2048], P('tp'), may hold values from -0.0625 to 0.0625
- root_cache: bfloat16 [8, 4096, 2, 2048], P(None, 'req', None, 'tp'), may hold values from -240 to 240
- mid_cache: bfloat16 [16, 2048, 2, 2048], P('req', None, None, 'tp'), may hold values from -240 to 240
- leaf_cache: bfloat16 [512, 128, 2, 2048], P('req', None, None, 'tp'), may hold values from -240 to 240
- held_hidden: bfloat16 [16, 256, 2048], P('req', None, 'tp'), may hold values from -6 to 6
- recompute_rows: int32 [16, 256], P('req'), may hold values from 0 to 2047, as said below
- root_len: int32 [8], replicated, may hold values from 1024 to 4096
- mid_len: int32 [16], replicated, may hold values from 256 to 2048
- leaf_len: int32 [512], P('req'), may hold values from 1 to 128
- mid_parent: int32 [16], replicated, may hold values from 0 to 7
- leaf_parent: int32 [512], replicated, may hold values from 0 to 15
Outputs:
- layer_out: bfloat16 [512, 2048], P('req', 'tp')
Inputs may be any that keep to these rules, and one draw needn't show every extreme that they name: `recompute_rows`: the 256 slots of one middle node are distinct.
All inputs are finite; a program needn't handle non-finite values.
Results may differ from a plain program's by a relative error of at most 0.02.
The roundings to bfloat16 on the way count: a program that leaves them out, or rounds other values in their place, can miss the bound.
Values may be sent and summed in bfloat16 or wider, within the bound.
A program may use at most 192 MiB of HBM per device.

v0:
```python
import math
import jax
import jax.numpy as jnp
from jax import lax
from jax.sharding import PartitionSpec as P

D = 2048
HEAD_DIM = 64
EPSILON = 1e-05
THETA_BASE = 130000.0
NEG_FILL = -1e30


def combined_all(value, axis, combine):
    everything = jax.tree.map(lambda part: lax.all_gather(part, axis), value)
    first = jax.tree.map(lambda part: part[0], everything)

    def lap(k, so_far):
        return combine(so_far, jax.tree.map(lambda part: part[k], everything))

    return lax.fori_loop(1, lax.axis_size(axis), lap, first)


def rms_scale(values, gain):
    return (
        values
        * lax.rsqrt(jnp.mean(values * values, axis=-1, keepdims=True) + EPSILON)
        * gain.astype(jnp.float32)
    )


def rotate(values, positions):
    half_dim = values.shape[-1] // 2
    inv_freq = jnp.exp(
        jnp.arange(half_dim, dtype=jnp.float32) * (-2.0 * math.log(THETA_BASE) / values.shape[-1])
    )
    angles = positions.astype(jnp.float32)[..., None, None] * inv_freq
    cosines = jnp.cos(angles)
    sines = jnp.sin(angles)
    leading = values[..., :half_dim]
    trailing = values[..., half_dim:]
    return jnp.concatenate(
        [leading * cosines - trailing * sines, trailing * cosines + leading * sines], axis=-1
    )


def lookup(table_values, indices):
    hits = indices[..., None] == jnp.arange(table_values.shape[0], dtype=jnp.int32)
    return jnp.sum(jnp.where(hits, table_values, 0), axis=-1)


def partial_softmax(queries, key_rows, live_mask, score_scale):
    count = key_rows.shape[0]
    heads = queries.shape[1]
    key_part = key_rows[:, 0].reshape(count, heads, HEAD_DIM)
    value_part = key_rows[:, 1].reshape(count, heads, HEAD_DIM)
    scores = (
        jnp.einsum("bhd,khd->hbk", queries, key_part, preferred_element_type=jnp.float32)
        * score_scale
    )
    live = live_mask[None]
    row_max = jnp.max(jnp.where(live, scores, NEG_FILL), axis=2)
    weights = jnp.where(live, jnp.exp(scores - row_max[..., None]), 0.0)
    row_sum = jnp.sum(weights, axis=2)
    weighted = jnp.einsum(
        "hbk,khd->bhd", weights.astype(jnp.bfloat16), value_part, preferred_element_type=jnp.float32
    )
    return (row_max.T, row_sum.T, weighted.reshape(queries.shape[0], heads * HEAD_DIM))


def join(earlier, latter):
    best = jnp.maximum(earlier[0], latter[0])
    factor_one = jnp.exp(earlier[0] - best)
    factor_two = jnp.exp(latter[0] - best)
    row_sum = earlier[1] * factor_one + latter[1] * factor_two
    weighted = earlier[2] * jnp.repeat(factor_one, HEAD_DIM, axis=1) + latter[2] * jnp.repeat(
        factor_two, HEAD_DIM, axis=1
    )
    return (best, row_sum, weighted)


def leaf_softmax(queries, leaf_cache, leaf_len, score_scale):
    own_rows, slots = leaf_cache.shape[:2]
    heads = queries.shape[1]
    key_part = leaf_cache[:, :, 0].reshape(own_rows, slots, heads, HEAD_DIM)
    value_part = leaf_cache[:, :, 1].reshape(own_rows, slots, heads, HEAD_DIM)
    scores = (
        jnp.einsum("rhd,rkhd->rhk", queries, key_part, preferred_element_type=jnp.float32)
        * score_scale
    )
    live = (jnp.arange(slots, dtype=jnp.int32)[None, :] < leaf_len[:, None])[:, None, :]
    row_max = jnp.max(jnp.where(live, scores, NEG_FILL), axis=2)
    weights = jnp.where(live, jnp.exp(scores - row_max[..., None]), 0.0)
    row_sum = jnp.sum(weights, axis=2)
    weighted = jnp.einsum(
        "rhk,rkhd->rhd",
        weights.astype(jnp.bfloat16),
        value_part,
        preferred_element_type=jnp.float32,
    )
    return (row_max, row_sum, weighted)


def on_device(
    stream,
    attn_gain,
    mlp_gain,
    w_query,
    w_keyval,
    w_out,
    w_gate_up,
    w_down,
    root_cache,
    mid_cache,
    leaf_cache,
    held_hidden,
    recompute_rows,
    root_len,
    mid_len,
    leaf_len,
    mid_parent,
    leaf_parent,
):
    req_rank = lax.axis_index("req")
    own_rows = stream.shape[0]
    query_width = w_query.shape[1]
    local_heads = query_width // HEAD_DIM
    score_scale = HEAD_DIM ** (-0.5)
    requests = leaf_parent.shape[0]
    all_roots = lookup(mid_parent, leaf_parent)
    own_mids = lax.dynamic_slice_in_dim(leaf_parent, req_rank * own_rows, own_rows)
    own_roots = lax.dynamic_slice_in_dim(all_roots, req_rank * own_rows, own_rows)
    positions = lookup(root_len, own_roots) + lookup(mid_len, own_mids) + leaf_len
    stream_float = stream.astype(jnp.float32)
    normed = rms_scale(stream_float, attn_gain).astype(jnp.bfloat16)
    keyval_flat = w_keyval.reshape(D, 2 * query_width)
    queries = rotate(
        jnp.dot(normed, w_query, preferred_element_type=jnp.float32).reshape(
            own_rows, local_heads, HEAD_DIM
        ),
        positions,
    ).astype(jnp.bfloat16)
    fresh = jnp.dot(normed, keyval_flat, preferred_element_type=jnp.float32).reshape(
        own_rows, 2, local_heads, HEAD_DIM
    )
    key_new = rotate(fresh[:, 0], positions).astype(jnp.bfloat16)
    value_new = fresh[:, 1].astype(jnp.bfloat16)
    node_count, slots = mid_cache.shape[:2]
    recomp_count = recompute_rows.shape[1]
    held = lax.all_gather(held_hidden, "tp", axis=2, tiled=True)
    held_normed = rms_scale(held.astype(jnp.float32), attn_gain).astype(jnp.bfloat16)
    rebuilt = jnp.dot(
        held_normed.reshape(node_count * recomp_count, D),
        keyval_flat,
        preferred_element_type=jnp.float32,
    ).reshape(node_count, recomp_count, 2, local_heads, HEAD_DIM)
    own_nodes = req_rank * node_count + jnp.arange(node_count, dtype=jnp.int32)
    own_lens = lax.dynamic_slice_in_dim(mid_len, req_rank * node_count, node_count)
    own_parents = lax.dynamic_slice_in_dim(mid_parent, req_rank * node_count, node_count)
    rebuilt_pos = lookup(root_len, own_parents)[:, None] + recompute_rows
    rebuilt = (
        jnp.stack([rotate(rebuilt[:, :, 0], rebuilt_pos), rebuilt[:, :, 1]], axis=2)
        .astype(jnp.bfloat16)
        .reshape(node_count * recomp_count, 2, query_width)
    )
    all_queries = lax.all_gather(
        queries.reshape(own_rows, query_width), "req", axis=0, tiled=True
    ).reshape(requests, local_heads, HEAD_DIM)
    root_count, slice_len = root_cache.shape[:2]
    token_ids = req_rank * slice_len + jnp.arange(slice_len, dtype=jnp.int32)
    root_valid = token_ids[None, :] < root_len[:, None]
    root_match = all_roots[:, None] == jnp.arange(root_count, dtype=jnp.int32)[None, :]
    root_mask = (root_match[:, :, None] & root_valid[None]).reshape(
        requests, root_count * slice_len
    )
    root_part = partial_softmax(
        all_queries,
        root_cache.reshape(root_count * slice_len, 2, query_width),
        root_mask,
        score_scale,
    )
    replaced = jnp.any(
        recompute_rows[:, :, None] == jnp.arange(slots, dtype=jnp.int32)[None, None, :], axis=1
    )
    slot_live = (jnp.arange(slots, dtype=jnp.int32)[None, :] < own_lens[:, None]) & jnp.logical_not(
        replaced
    )
    belongs = leaf_parent[:, None] == own_nodes[None, :]
    held_mask = (belongs[:, :, None] & slot_live[None]).reshape(requests, node_count * slots)
    fresh_mask = (belongs[:, :, None] & (recompute_rows < own_lens[:, None])[None]).reshape(
        requests, node_count * recomp_count
    )
    mid_keys = jnp.concatenate(
        [mid_cache.reshape(node_count * slots, 2, query_width), rebuilt], axis=0
    )
    mid_part = partial_softmax(
        all_queries, mid_keys, jnp.concatenate([held_mask, fresh_mask], axis=1), score_scale
    )
    part_max, part_sum, part_acc = join(root_part, mid_part)
    merged_max, merged_sum, merged_acc = combined_all((part_max, part_sum, part_acc), "req", join)
    remote_max = lax.dynamic_slice_in_dim(merged_max, req_rank * own_rows, own_rows, 0)[None]
    remote_sum = lax.dynamic_slice_in_dim(merged_sum, req_rank * own_rows, own_rows, 0)[None]
    remote_acc = lax.dynamic_slice_in_dim(merged_acc, req_rank * own_rows, own_rows, 0)[None]
    leaf_max, leaf_sum, leaf_acc = leaf_softmax(queries, leaf_cache, leaf_len, score_scale)
    self_score = (
        jnp.sum(queries.astype(jnp.float32) * key_new.astype(jnp.float32), axis=-1) * score_scale
    )
    best = jnp.maximum(jnp.maximum(jnp.max(remote_max, axis=0), leaf_max), self_score)
    remote_factor = jnp.exp(remote_max - best[None])
    leaf_factor = jnp.exp(leaf_max - best)
    self_factor = jnp.exp(self_score - best)
    row_sum = jnp.sum(remote_sum * remote_factor, axis=0) + leaf_sum * leaf_factor + self_factor
    sources = remote_acc.shape[0]
    weighted = jnp.sum(
        remote_acc.reshape(sources, own_rows, local_heads, HEAD_DIM) * remote_factor[..., None],
        axis=0,
    )
    weighted = (
        weighted
        + leaf_acc * leaf_factor[..., None]
        + value_new.astype(jnp.float32) * self_factor[..., None]
    )
    attended = (weighted / row_sum[..., None]).reshape(own_rows, query_width).astype(jnp.bfloat16)
    attn_part = jnp.dot(attended, w_out, preferred_element_type=jnp.float32)
    width_share = D // lax.axis_size("tp")
    tp_rank = lax.axis_index("tp")
    residual = stream_float + lax.psum(attn_part, "tp")
    mixed_in = rms_scale(residual, mlp_gain).astype(jnp.bfloat16)
    residual_share = lax.dynamic_slice_in_dim(residual, tp_rank * width_share, width_share, 1)
    hidden_width = w_gate_up.shape[2]
    projected = jnp.dot(
        mixed_in, w_gate_up.reshape(D, 2 * hidden_width), preferred_element_type=jnp.float32
    ).reshape(own_rows, 2, hidden_width)
    hidden = (jax.nn.silu(projected[:, 0]) * projected[:, 1]).astype(jnp.bfloat16)
    down_share = lax.psum_scatter(
        jnp.dot(hidden, w_down, preferred_element_type=jnp.float32),
        "tp",
        scatter_dimension=1,
        tiled=True,
    )
    return (residual_share + down_share).astype(jnp.bfloat16)


def solution(mesh):
    placed = (
        P("req", None),
        P(),
        P(),
        P(None, "tp"),
        P(None, None, "tp"),
        P("tp", None),
        P(None, None, "tp"),
        P("tp", None),
        P(None, "req", None, "tp"),
        P("req", None, None, "tp"),
        P("req", None, None, "tp"),
        P("req", None, "tp"),
        P("req", None),
        P(),
        P(),
        P("req"),
        P(),
        P(),
    )
    return jax.shard_map(
        on_device, mesh=mesh, in_specs=placed, out_specs=P("req", "tp"), check_vma=False
    )
```

profile of v0, /device:TPU:0, one launch (start us, length us, event | category | flops | bytes accessed | tf_op | source)
XLA Modules:
  0.0 369.5 jit_solution(2306715656610677094)
XLA Ops:
  9.8 1.3 dynamic_slice.57
  11.1 1.2 dynamic_slice.56
  14.8 1.6 fusion.62
  16.6 2.1 copy.109
  18.7 2.5 copy.77
  21.2 2.8 fusion.44
  26.2 24.1 %all_gather.22 = bf16[512,256]{1,0:T(8,128)(2,1)S(1)} all-gather(bf16[32,256]{1,0:T(8,128)(2,1)S(1)} %convert_element_type.81), channel_id=1, replica_groups=mesh['req'=16,'tp'=8] {'req'}, dimensions={0}, use_global_device_ids=true | all-gather | bytes 278528 | tf_op jit(solution)/shard_map/all_gather | solution.py:166
  51.2 1.8 and.64
  53.0 1.6 copy.107
  54.6 4.2 %fusion.81 = (bf16[2048,1,256]{2,1,0:T(2,128)(2,1)}, bf16[2048,1,256]{2,1,0:T(2,128)(2,1)}) fusion(bf16[2048,2,256]{2,1,0:T(2,128)(2,1)S(1)} %bitcast.183), kind=kLoop, calls=%fused_computation.143 | loop fusion | bytes 4194304 | tf_op jit(solution)/shard_map/slice | solution.py:56
  58.8 6.0 %copy.103 = bf16[2048,1,256]{0,2,1:T(8,128)(2,1)} copy(bf16[2048,1,256]{2,1,0:T(2,128)(2,1)} %get-tuple-element.234) | data formatting | bytes 2097152
  64.8 1.3 fusion.70
  69.3 1.5 broadcast_and_fusion
  71.6 4.3 %copy.104 = bf16[2048,1,256]{0,2,1:T(8,128)(2,1)} copy(bf16[2048,1,256]{2,1,0:T(2,128)(2,1)S(1)} %copy-done.4) | data formatting | bytes 2097152
  75.9 1.9 broadcast_and_fusion.1
  77.9 2.5 pad_add_fusion
  80.3 4.5 %select_reduce_fusion.1 = (f32[4,512]{1,0:T(4,128)S(1)}, f32[4,512,2048]{2,1,0:T(8,128)S(1)}) fusion(pred[512,2048]{1,0:T(8,128)(4,1)S(1)} %broadcast_and_fusion.1, bf16[512,4,64]{0,2,1:T(8,128)(2,1)} %bitcast.189, bf16[2048,4,64]{0,2,1:T(8,128)(2,1)S(1)} %bitcast.188), kind=kOutput, calls=%fused_computation.13 | convolution fusion | flops 549451776 | bytes 19144704 | tf_op jit(solution)/shard_map/bhd,khd->hbk/dot_general | solution.py:58
  84.9 5.7 %copy-done.1 = f32[4,512,2048]{2,1,0:T(8,128)} copy-done((f32[4,512,2048]{2,1,0:T(8,128)}, f32[4,512,2048]{2,1,0:T(8,128)S(1)}, u32[]{:S(2)}) %copy-start.1) | copy-done | bytes 16777240
  90.6 5.2 %fusion.6 = f32[4,512]{1,0:T(4,128)} fusion(f32[4,512,2048]{2,1,0:T(8,128)S(1)} %get-tuple-element.253, f32[4,512]{1,0:T(4,128)S(1)} %get-tuple-element.252, pred[512,2048]{1,0:T(8,128)(4,1)S(1)} %broadcast_and_fusion.1), kind=kLoop, calls=%fused_computation.17 | loop fusion | flops 16775168 | bytes 17842176 | tf_op jit(solution)/shard_map/reduce_sum | solution.py:64
  95.8 1.5 fusion.13
  97.3 2.8 convolution_bitcast_fusion
  100.6 13.3 %maximum_maximum_fusion = bf16[2304,2,256]{2,1,0:T(2,128)(2,1)S(1)} fusion(bf16[256,1,256]{2,1,0:T(2,128)(2,1)S(1)} %copy.79, bf16[256,1,256]{2,1,0:T(2,128)(2,1)S(1)} %copy.78, bf16[2048,2,256]{2,1,0:T(2,128)(2,1)} %bitcast.196), kind=kLoop, calls=%fused_computation.25 | loop fusion | flops 7077888 | bytes 4718592 | tf_op jit(solution)/shard_map/concatenate | solution.py:193
  113.9 4.8 %fusion.80 = (bf16[2304,1,256]{2,1,0:T(2,128)(2,1)}, bf16[2304,1,256]{2,1,0:T(2,128)(2,1)}) fusion(bf16[2304,2,256]{2,1,0:T(2,128)(2,1)S(1)} %maximum_maximum_fusion), kind=kLoop, calls=%fused_computation.142 | loop fusion | bytes 4718592 | tf_op jit(solution)/shard_map/slice | solution.py:56
  118.7 6.0 %copy.80 = bf16[2304,1,256]{0,2,1:T(8,128)(2,1)} copy(bf16[2304,1,256]{2,1,0:T(2,128)(2,1)} %get-tuple-element.232) | data formatting | bytes 2359296 | tf_op jit(solution)/shard_map/slice | solution.py:55
  124.7 6.0 %copy.82 = bf16[2304,1,256]{0,2,1:T(8,128)(2,1)} copy(bf16[2304,1,256]{2,1,0:T(2,128)(2,1)} %get-tuple-element.231) | data formatting | bytes 2359296 | tf_op jit(solution)/shard_map/slice | solution.py:56
  130.7 5.6 %select_reduce_fusion = (f32[4,512]{1,0:T(4,128)S(1)}, f32[4,512,2304]{2,1,0:T(8,128)S(1)}) fusion(pred[512,2304]{1,0:T(8,128)(4,1)} %pad_add_fusion, bf16[512,4,64]{0,2,1:T(8,128)(2,1)} %bitcast.190, bf16[2304,4,64]{0,2,1:T(8,128)(2,1)} %bitcast.187), kind=kOutput, calls=%fused_computation.11 | convolution fusion | flops 618133504 | bytes 21504000 | tf_op jit(solution)/shard_map/bhd,khd->hbk/dot_general | solution.py:58
  136.4 5.1 %fusion.4 = f32[4,512]{1,0:T(4,128)S(1)} fusion(f32[4,512,2304]{2,1,0:T(8,128)S(1)} %get-tuple-element.251, f32[4,512]{1,0:T(4,128)S(1)} %get-tuple-element.250, pred[512,2304]{1,0:T(8,128)(4,1)S(1)} %copy-done.2), kind=kLoop, calls=%fused_computation.15 | loop fusion | flops 18872320 | bytes 20070400 | tf_op jit(solution)/shard_map/reduce_sum | solution.py:64
  142.1 6.8 %fusion.29 = f32[512,4,64]{0,2,1:T(8,128)} fusion(bf16[2304,4,64]{0,2,1:T(8,128)(2,1)} %bitcast.197, f32[4,512,2304]{2,1,0:T(8,128)S(1)} %get-tuple-element.251, f32[4,512]{1,0:T(4,128)S(1)} %get-tuple-element.250, pred[512,2304]{1,0:T(8,128)(4,1)} %pad_add_fusion, f32[512,4]{0,1:T(4,128)} %get-tuple-element.228), kind=kOutput, calls=%fused_computation.38 | convolution fusion | flops 622985216 | bytes 21774336 | tf_op jit(solution)/shard_map/hbk,khd->bhd/dot_general | solution.py:65
  148.9 8.0 %fusion.26 = f32[512,4,64]{0,2,1:T(8,128)S(1)} fusion(f32[512,4,64]{0,2,1:T(8,128)} %fusion.29, bf16[2048,4,64]{0,2,1:T(8,128)(2,1)} %bitcast.198, f32[4,512,2048]{2,1,0:T(8,128)} %copy-done.1, f32[4,512]{1,0:T(4,128)S(1)} %copy-done.14, pred[512,2048]{1,0:T(8,128)(4,1)S(1)} %broadcast_and_fusion.1, f32[512,4]{0,1:T(4,128)S(1)} %get-tuple-element.227), kind=kOutput, calls=%fused_computation.37 | convolution fusion | flops 553910272 | bytes 19939328 | tf_op jit(solution)/shard_map/hbk,khd->bhd/dot_general | solution.py:65
  158.0 10.0 %fusion.79 = (bf16[32,128,1,256]{3,2,1,0:T(2,128)(2,1)}, bf16[32,128,1,256]{3,2,1,0:T(2,128)(2,1)}) fusion(bf16[32,128,2,256]{3,2,1,0:T(2,128)(2,1)} %param.30), kind=kLoop, calls=%fused_computation.141 | loop fusion | bytes 8388608 | tf_op jit(solution)/shard_map/slice | solution.py:85
  168.0 9.8 %copy.105 = bf16[32,128,1,256]{1,3,0,2:T(8,128)(2,1)} copy(bf16[32,128,1,256]{3,2,1,0:T(2,128)(2,1)} %get-tuple-element.229) | data formatting | bytes 4194304
  177.8 8.6 %copy.106 = bf16[32,128,1,256]{1,3,0,2:T(8,128)(2,1)S(1)} copy(bf16[32,128,1,256]{3,2,1,0:T(2,128)(2,1)} %get-tuple-element.230) | data formatting | bytes 4194304
  186.5 2.2 fusion.56
  189.0 1.2 fusion.54
  190.2 23.4 %all-gather = f32[8192,4]{0,1:T(4,128)S(1)} all-gather(f32[512,4]{0,1:T(4,128)S(1)} %get-tuple-element.245), channel_id=2, replica_groups=mesh['req'=16,'tp'=8] {'req'}, dimensions={0}, use_global_device_ids=true | all-gather | bytes 139264 | tf_op jit(solution)/shard_map/all_gather | solution.py:15
  213.6 21.6 %all-gather.1 = f32[8192,4]{0,1:T(4,128)S(1)} all-gather(f32[512,4]{0,1:T(4,128)S(1)} %get-tuple-element.226), channel_id=3, replica_groups=mesh['req'=16,'tp'=8] {'req'}, dimensions={0}, use_global_device_ids=true | all-gather | bytes 139264 | tf_op jit(solution)/shard_map/all_gather | solution.py:15
  236.5 23.7 %while.19 = (s32[]{:T(128)}, f32[512,4]{0,1:T(4,128)S(1)}, f32[512,4]{0,1:T(4,128)S(1)}, f32[512,256]{0,1:T(8,128)S(1)}, f32[16,512,4]{1,2,0:T(4,128)S(1)}, /*in...) while((s32[]{:T(128)}, f32[512,4]{0,1:T(4,128)S(1)}, ...), condition=%wide.region_12.13_spmd, body=%wide.region_11.12_spmd.sunk | while | flops 405509 | bytes 3752087 | solution.py:21
  236.6 1.1 constant_dynamic-slice_fusion.3
  239.7 1.1 constant_dynamic-slice_fusion.3
  241.3 1.1 constant_dynamic-slice_fusion.3
  262.7 10.1 %copy.110 = bf16[256,8,2,1024]{3,1,2,0:T(8,128)(2,1)} copy(bf16[256,8,2,1024]{3,2,1,0:T(2,128)(2,1)} %bitcast.182) | data formatting | bytes 16777216
  272.8 12.4 %copy.91 = bf16[2048,2048]{1,0:T(8,128)(2,1)} copy(bf16[2048,2048]{0,1:T(8,128)(2,1)} %bitcast.181) | data formatting | bytes 16777216 | tf_op jit(solution)/shard_map/dot_general | solution.py:231
  285.2 37.8 %all-reduce.2.cloned.1.call-done = f32[32,2048]{1,0:T(8,128)} async-done(((f32[32,2048]{1,0:T(8,128)}), f32[32,2048]{1,0:T(8,128)}) %all-reduce.2.cloned.1.call-update) | async-done | bytes 262160 | tf_op jit(solution)/shard_map/psum | solution.py:227
  323.0 1.1 multiply_reduce_fusion
  324.1 6.1 %fusion.40 = f32[32,2,1024]{2,0,1:T(8,128)S(1)} fusion(bf16[2,1024,2048]{2,1,0:T(8,128)(2,1)} %bitcast.180, f32[32,2048]{1,0:T(8,128)S(1)} %get-tuple-element.219, f32[2048]{0:T(1024)S(1)} %convert_element_type.94, f32[32]{0:T(128)S(1)} %add_rsqrt_fusion.1), kind=kOutput, calls=%fused_computation.56 | convolution fusion | flops 268632064 | bytes 8921216 | tf_op jit(solution)/shard_map/dot_general | solution.py:231
  330.2 1.5 fusion.48
  331.8 29.8 %reduce-scatter.2.cloned.1.call-done = f32[32,256]{1,0:T(8,128)} async-done(((f32[32,2048]{1,0:T(8,128)}), f32[32,256]{1,0:T(8,128)}) %reduce-scatter.2.cloned.1.call-update) | async-done | bytes 32784 | tf_op jit(solution)/shard_map/reduce_scatter | solution.py:235
  361.6 1.4 add_convert_fusion.2
  (168 shorter events, 39.1 us)
Async XLA Ops:
  6.5 255.1 %copy-start = (bf16[256,2048]{1,0:T(8,128)(2,1)S(1)}, bf16[256,2048]{1,0:T(8,128)(2,1)}, u32[]{:S(2)}) copy-start(bf16[256,2048]{1,0:T(8,128)(2,1)} %param.25) | copy-start | bytes 3145732
  6.5 89.2 %all-gather.5.cloned.1.call-start = ((), (), s32[]{:S(2)}) async-start(), calls=%async_computation.1 | async-start | bytes 1179648 | tf_op jit(solution)/shard_map/all_gather | solution.py:150
  7.3 228.0 %all-gather.7.cloned.1.call-start = ((), (), s32[]{:S(2)}) async-start(), calls=%async_computation.2 | async-start | bytes 8912896 | tf_op jit(solution)/shard_map/all_gather | solution.py:15
  16.6 4.6 %copy-start.7 = (bf16[32,2048]{1,0:T(8,128)(2,1)S(1)}, bf16[32,2048]{1,0:T(8,128)(2,1)}, u32[]{:S(2)}) copy-start(bf16[32,2048]{1,0:T(8,128)(2,1)} %param.20) | copy-start | bytes 393220
  18.7 5.4 %copy-start.21 = (s32[8]{0:T(128)S(1)}, s32[8]{0:T(128)}, u32[]{:S(2)}) copy-start(s32[8]{0:T(128)} %param.33) | copy-start | bytes 100
  18.7 5.5 %copy-start.19 = (s32[32]{0:T(128)S(1)}, s32[32]{0:T(128)}, u32[]{:S(2)}) copy-start(s32[32]{0:T(128)} %param.35) | copy-start | bytes 388
  21.2 33.4 %copy-start.3 = (bf16[8,256,2,256]{3,2,1,0:T(2,128)(2,1)S(1)}, bf16[8,256,2,256]{3,2,1,0:T(2,128)(2,1)}, u32[]{:S(2)}) copy-start(bf16[8,256,2,256]{3,2,1,0:T(2,128)(2,1)} %param.28) | copy-start | bytes 6291460
  24.1 0.7 copy-start.9
  25.5 0.6 copy-start.11
  54.6 11.5 %copy-start.18 = (s32[1,256]{1,0:T(1,128)S(1)}, s32[1,256]{1,0:T(1,128)}, u32[]{:S(2)}) copy-start(s32[1,256]{1,0:T(1,128)} %param.32) | copy-start | bytes 3076
  58.8 12.8 %copy-start.4 = (bf16[2048,1,256]{2,1,0:T(2,128)(2,1)S(1)}, bf16[2048,1,256]{2,1,0:T(2,128)(2,1)}, u32[]{:S(2)}) copy-start(bf16[2048,1,256]{2,1,0:T(2,128)(2,1)} %get-tuple-element.233) | copy-start | bytes 3145732
  75.9 4.5 %copy-start.5 = (bf16[2048,1,256]{0,2,1:T(8,128)(2,1)S(1)}, bf16[2048,1,256]{0,2,1:T(8,128)(2,1)}, u32[]{:S(2)}) copy-start(bf16[2048,1,256]{0,2,1:T(8,128)(2,1)} %copy.103) | copy-start | bytes 3145732
  84.9 5.7 %copy-start.1 = (f32[4,512,2048]{2,1,0:T(8,128)}, f32[4,512,2048]{2,1,0:T(8,128)S(1)}, u32[]{:S(2)}) copy-start(f32[4,512,2048]{2,1,0:T(8,128)S(1)} %get-tuple-element.253) | copy-start | bytes 50331652
  84.9 5.7 %copy-start.13 = (f32[4,512]{1,0:T(4,128)}, f32[4,512]{1,0:T(4,128)S(1)}, u32[]{:S(2)}) copy-start(f32[4,512]{1,0:T(4,128)S(1)} %get-tuple-element.252) | copy-start | bytes 24580
  95.8 4.3 %copy-start.10 = (f32[256,32]{0,1:T(8,128)S(1)}, f32[256,32]{0,1:T(8,128)}, u32[]{:S(2)}) copy-start(f32[256,32]{0,1:T(8,128)} %get-tuple-element.247) | copy-start | bytes 98308
  130.7 5.6 %copy-start.2 = (pred[512,2304]{1,0:T(8,128)(4,1)S(1)}, pred[512,2304]{1,0:T(8,128)(4,1)}, u32[]{:S(2)}) copy-start(pred[512,2304]{1,0:T(8,128)(4,1)} %pad_add_fusion) | copy-start | bytes 3538948
  136.4 5.1 %copy-start.14 = (f32[4,512]{1,0:T(4,128)S(1)}, f32[4,512]{1,0:T(4,128)}, u32[]{:S(2)}) copy-start(f32[4,512]{1,0:T(4,128)} %copy-done.13) | copy-start | bytes 24580
  136.4 5.1 %copy-start.15 = (f32[4,512]{1,0:T(4,128)S(1)}, f32[4,512]{1,0:T(4,128)}, u32[]{:S(2)}) copy-start(f32[4,512]{1,0:T(4,128)} %fusion.6) | copy-start | bytes 24580
  157.9 165.1 %all-reduce.2.cloned.1.call-start = ((), (), s32[]{:S(2)}) async-start(), calls=%async_computation.3 | async-start | bytes 524288 | tf_op jit(solution)/shard_map/psum | solution.py:227
  177.8 8.6 %copy-start.20 = (s32[32]{0:T(128)S(1)}, s32[32]{0:T(128)}, u32[]{:S(2)}) copy-start(s32[32]{0:T(128)} %param.35) | copy-start | bytes 388
  177.8 8.7 %copy-start.12 = (bf16[32,4,64]{2,0,1:T(8,128)(2,1)S(1)}, bf16[32,4,64]{2,0,1:T(8,128)(2,1)}, u32[]{:S(2)}) copy-start(bf16[32,4,64]{2,0,1:T(8,128)(2,1)} %copy-done.11) | copy-start | bytes 49156
  236.5 23.9 %copy-start.16 = (f32[32,4]{0,1:T(4,128)S(1)}, f32[32,4]{0,1:T(4,128)}, u32[]{:S(2)}) copy-start(f32[32,4]{0,1:T(4,128)} %get-tuple-element.224) | copy-start | bytes 1540
  262.6 99.0 %reduce-scatter.2.cloned.1.call-start = ((), (), s32[]{:S(2)}) async-start(), calls=%async_computation.4 | async-start | bytes 294912 | tf_op jit(solution)/shard_map/reduce_scatter | solution.py:235
  272.8 12.4 %copy-start.17 = (bf16[2048]{0:T(1024)(128)(2,1)S(1)}, bf16[2048]{0:T(1024)(128)(2,1)}, u32[]{:S(2)}) copy-start(bf16[2048]{0:T(1024)(128)(2,1)} %param.22) | copy-start | bytes 12292
  272.8 50.2 %copy-start.8 = (bf16[32,2048]{1,0:T(8,128)(2,1)S(1)}, bf16[32,2048]{1,0:T(8,128)(2,1)}, u32[]{:S(2)}) copy-start(bf16[32,2048]{1,0:T(8,128)(2,1)} %param.20) | copy-start | bytes 393220
  324.1 6.2 %copy-start.6 = (bf16[1024,2048]{1,0:T(8,128)(2,1)S(1)}, bf16[1024,2048]{1,0:T(8,128)(2,1)}, u32[]{:S(2)}) copy-start(bf16[1024,2048]{1,0:T(8,128)(2,1)} %param.27) | copy-start | bytes 12582916
Sparse Core Ops, SparseCore 0:
  9.0 26.0 all-gather.4
  158.0 71.9 all-gather.6
  262.7 60.1 all-reduce.1
  331.9 29.6 reduce-scatter.1
where the time goes:
time: 372 us; the launch traced here: 370 us
  local copies, waits for them, and re-layouts  124 us (33%)
  blocking collectives  69.1 us (19%)
  waiting for transfers between devices  68.4 us (18%)
  other arithmetic  50 us (13%)
  matrix products  44.2 us (12%)
  between operations  13.5 us (4%)
    unnamed x53, local copies, waits for them, and re-layouts  49.1 us
    all_gather x2, blocking collectives, combined_all(): everything = jax.tree.map(lambda part: lax.all_gather(part, axis), value)  45 us
    psum x1, waiting for transfers between devices, on_device(): residual = stream_float + lax.psum(attn_part, 'tp')  37.8 us
    reduce_scatter x1, waiting for transfers between devices, on_device(): lax.psum_scatter(jnp.dot(hidden, w_down, preferred_element_type=jnp.float...  29.8 us
    all_gather x1, blocking collectives, on_device(): lax.all_gather(queries.reshape(own_rows, query_width), 'req', axis=0, til...  24.1 us
    dynamic_slice x30, local copies, waits for them, and re-layouts, lap(): return combine(so_far, jax.tree.map(lambda part: part[k], everything))  19.2 us
    slice x3, local copies, waits for them, and re-layouts, partial_softmax(): value_part = key_rows[:, 1].reshape(count, heads, HEAD_DIM)  15 us
    dot_general x2, matrix products, partial_softmax(): jnp.einsum('hbk,khd->bhd', weights.astype(jnp.bfloat16), value_part, pref...  14.8 us
  transfers between devices with their start and end apart: 4, of which 2 were waited for; matrix products, arithmetic and copies ran while one was open for 30% of the time, Pallas kernels for 0%

commit v1 on v0

--- a/solution.py
+++ b/solution.py
@@ -163,8 +163,11 @@
         .astype(jnp.bfloat16)
         .reshape(node_count * recomp_count, 2, query_width)
     )
-    all_queries = lax.all_gather(
-        queries.reshape(own_rows, query_width), "req", axis=0, tiled=True
+    all_queries = jnp.concatenate(
+        lax.all_to_all(
+            jnp.stack([queries.reshape(own_rows, query_width)] * lax.axis_size("req")), "req", 0, 0
+        ),
+        axis=0,
     ).reshape(requests, local_heads, HEAD_DIM)
     root_count, slice_len = root_cache.shape[:2]
     token_ids = req_rank * slice_len + jnp.arange(slice_len, dtype=jnp.int32)

time: 372 us -> 354 us (0.952)
  blocking collectives: 69.1 us -> 47.3 us
  starting transfers between devices: 0.13 us -> 7.62 us
  other arithmetic: 50 us -> 44.5 us
    all_gather x1 -> x0, blocking collectives: 24.1 us -> none  [on_device(): lax.all_gather(queries.reshape(own_rows, query_width), 'req', axis=0, til...]
    all_to_all x0 -> x1, starting transfers between devices: none -> 7.17 us  [on_device(): lax.all_to_all(jnp.stack([queries.reshape(own_rows, query_width)] * lax.a...]
    another operation x0 -> x3, local copies, waits for them, and re-layouts: none -> 4.08 us  [the longest x2 3.33 us: on_device(): all_queries = jnp.concatenate(lax.all_to_all(jnp.stack([queries.reshape(o...]
    unnamed x53 -> x59, local copies, waits for them, and re-layouts: 49.1 us -> 47.7 us
  transfers between devices with their start and end apart: 4 -> 5, of which waited for: 2 -> 2; matrix products, arithmetic and copies ran while one was open for 30% -> 26% of each run, Pallas kernels for 0% -> 0%
where the time goes in v1:
time: 354 us; the launch traced here: 349 us
  local copies, waits for them, and re-layouts  124 us (35%)
  waiting for transfers between devices  67.6 us (19%)
  blocking collectives  47.3 us (13%)
  other arithmetic  44.5 us (13%)
  matrix products  43.1 us (12%)
  between operations  13.9 us (4%)
  starting transfers between devices  7.62 us (2%)
    unnamed x59, local copies, waits for them, and re-layouts  47.7 us
    all_gather x2, blocking collectives, combined_all(): everything = jax.tree.map(lambda part: lax.all_gather(part, axis), value)  47.3 us
    psum x1, waiting for transfers between devices, on_device(): residual = stream_float + lax.psum(attn_part, 'tp')  37 us
    reduce_scatter x1, waiting for transfers between devices, on_device(): lax.psum_scatter(jnp.dot(hidden, w_down, preferred_element_type=jnp.float...  29.8 us
    dynamic_slice x30, local copies, waits for them, and re-layouts, lap(): return combine(so_far, jax.tree.map(lambda part: part[k], everything))  19.2 us
    slice x3, local copies, waits for them, and re-layouts, partial_softmax(): value_part = key_rows[:, 1].reshape(count, heads, HEAD_DIM)  15.1 us
    dot_general x2, matrix products, partial_softmax(): jnp.einsum('hbk,khd->bhd', weights.astype(jnp.bfloat16), value_part, pref...  15 us
    concatenate x1, other arithmetic, on_device(): jnp.concatenate([mid_cache.reshape(node_count * slots, 2, query_width), r...  13.8 us
  transfers between devices with their start and end apart: 5, of which 2 were waited for; matrix products, arithmetic and copies ran while one was open for 26% of the time, Pallas kernels for 0%

profile of v1, /device:TPU:0, one launch (start us, length us, event | category | flops | bytes accessed | tf_op | source)
XLA Modules:
  0.0 348.6 jit_solution(2424717255625928734)
XLA Ops:
  10.0 1.6 fusion.62
  11.8 2.1 copy.112
  14.0 2.4 copy.79
  16.4 2.8 fusion.44
  21.6 7.2 %all-to-all-start = ((bf16[16,32,256]{2,1,0:T(8,128)(2,1)}), bf16[16,32,256]{2,1,0:T(8,128)(2,1)}, u32[]{:S(2)}, u32[]{:S(2)}) async-start(bf16[16,32,256]{2,1,0:T(8,128)(2,1)} %stack.11), calls=%async_computation | async-start | bytes 524288 | tf_op jit(solution)/shard_map/all_to_all | solution.py:167
  31.2 1.6 and.64
  33.5 4.2 %fusion.81 = (bf16[2048,1,256]{2,1,0:T(2,128)(2,1)}, bf16[2048,1,256]{2,1,0:T(2,128)(2,1)}) fusion(bf16[2048,2,256]{2,1,0:T(2,128)(2,1)S(1)} %bitcast.182), kind=kLoop, calls=%fused_computation.143 | loop fusion | bytes 4194304 | tf_op jit(solution)/shard_map/slice | solution.py:56
  37.7 1.3 fusion.70
  42.1 1.1 pad_add_fusion
  44.0 4.6 %copy.106 = bf16[2048,1,256]{0,2,1:T(8,128)(2,1)S(1)} copy(bf16[2048,1,256]{2,1,0:T(2,128)(2,1)} %get-tuple-element.234) | data formatting | bytes 2097152
  48.5 5.9 %copy.107 = bf16[2048,1,256]{0,2,1:T(8,128)(2,1)} copy(bf16[2048,1,256]{2,1,0:T(2,128)(2,1)} %get-tuple-element.233) | data formatting | bytes 2097152
  54.6 2.0 reshape_reshape.3
  56.6 1.3 copy.78
  57.9 3.3 select_reduce_fusion.1
  61.2 5.7 %copy-done.1 = f32[4,512,2048]{2,1,0:T(8,128)} copy-done((f32[4,512,2048]{2,1,0:T(8,128)}, f32[4,512,2048]{2,1,0:T(8,128)S(1)}, u32[]{:S(2)}) %copy-start.1) | copy-done | bytes 16777240
  66.9 5.2 %fusion.6 = f32[4,512]{1,0:T(4,128)} fusion(f32[4,512,2048]{2,1,0:T(8,128)S(1)} %get-tuple-element.253, f32[4,512]{1,0:T(4,128)S(1)} %get-tuple-element.252, pred[512,2048]{1,0:T(8,128)(4,1)S(1)} %broadcast_and_fusion.1), kind=kLoop, calls=%fused_computation.17 | loop fusion | flops 16775168 | bytes 17842176 | tf_op jit(solution)/shard_map/reduce_sum | solution.py:64
  72.1 1.5 fusion.13
  73.7 2.7 convolution_bitcast_fusion
  76.9 13.8 %maximum_maximum_fusion = bf16[2304,2,256]{2,1,0:T(2,128)(2,1)S(1)} fusion(bf16[256,1,256]{2,1,0:T(2,128)(2,1)S(1)} %copy.81, bf16[256,1,256]{2,1,0:T(2,128)(2,1)S(1)} %copy.80, bf16[2048,2,256]{2,1,0:T(2,128)(2,1)} %bitcast.193), kind=kLoop, calls=%fused_computation.25 | loop fusion | flops 7077888 | bytes 4718592 | tf_op jit(solution)/shard_map/concatenate | solution.py:196
  90.7 4.8 %fusion.80 = (bf16[2304,1,256]{2,1,0:T(2,128)(2,1)}, bf16[2304,1,256]{2,1,0:T(2,128)(2,1)}) fusion(bf16[2304,2,256]{2,1,0:T(2,128)(2,1)S(1)} %maximum_maximum_fusion), kind=kLoop, calls=%fused_computation.142 | loop fusion | bytes 4718592 | tf_op jit(solution)/shard_map/slice | solution.py:56
  95.5 6.0 %copy.82 = bf16[2304,1,256]{0,2,1:T(8,128)(2,1)} copy(bf16[2304,1,256]{2,1,0:T(2,128)(2,1)} %get-tuple-element.232) | data formatting | bytes 2359296 | tf_op jit(solution)/shard_map/slice | solution.py:55
  101.6 6.1 %copy.85 = bf16[2304,1,256]{0,2,1:T(8,128)(2,1)} copy(bf16[2304,1,256]{2,1,0:T(2,128)(2,1)} %get-tuple-element.231) | data formatting | bytes 2359296 | tf_op jit(solution)/shard_map/slice | solution.py:56
  107.6 5.6 %select_reduce_fusion = (f32[4,512]{1,0:T(4,128)S(1)}, f32[4,512,2304]{2,1,0:T(8,128)S(1)}) fusion(pred[512,2304]{1,0:T(8,128)(4,1)} %pad_add_fusion, bf16[512,4,64]{0,2,1:T(8,128)(2,1)} %copy-done.4, bf16[2304,4,64]{0,2,1:T(8,128)(2,1)} %bitcast.186), kind=kOutput, calls=%fused_computation.11 | convolution fusion | flops 618133504 | bytes 21504000 | tf_op jit(solution)/shard_map/bhd,khd->hbk/dot_general | solution.py:58
  113.3 5.1 %fusion.4 = f32[4,512]{1,0:T(4,128)S(1)} fusion(f32[4,512,2304]{2,1,0:T(8,128)S(1)} %get-tuple-element.251, f32[4,512]{1,0:T(4,128)S(1)} %get-tuple-element.250, pred[512,2304]{1,0:T(8,128)(4,1)S(1)} %copy-done.2), kind=kLoop, calls=%fused_computation.15 | loop fusion | flops 18872320 | bytes 20070400 | tf_op jit(solution)/shard_map/reduce_sum | solution.py:64
  119.0 6.8 %fusion.29 = f32[512,4,64]{0,2,1:T(8,128)} fusion(bf16[2304,4,64]{0,2,1:T(8,128)(2,1)} %bitcast.194, f32[4,512,2304]{2,1,0:T(8,128)S(1)} %get-tuple-element.251, f32[4,512]{1,0:T(4,128)S(1)} %get-tuple-element.250, pred[512,2304]{1,0:T(8,128)(4,1)} %pad_add_fusion, f32[512,4]{0,1:T(4,128)} %get-tuple-element.228), kind=kOutput, calls=%fused_computation.38 | convolution fusion | flops 622985216 | bytes 21774336 | tf_op jit(solution)/shard_map/hbk,khd->bhd/dot_general | solution.py:65
  125.8 8.2 %fusion.26 = f32[512,4,64]{0,2,1:T(8,128)S(1)} fusion(f32[512,4,64]{0,2,1:T(8,128)} %fusion.29, bf16[2048,4,64]{0,2,1:T(8,128)(2,1)} %bitcast.195, f32[4,512,2048]{2,1,0:T(8,128)} %copy-done.1, f32[4,512]{1,0:T(4,128)} %copy-done.9, pred[512,2048]{1,0:T(8,128)(4,1)S(1)} %broadcast_and_fusion.1, f32[512,4]{0,1:T(4,128)} %get-tuple-element.227), kind=kOutput, calls=%fused_computation.37 | convolution fusion | flops 553910272 | bytes 19939328 | tf_op jit(solution)/shard_map/hbk,khd->bhd/dot_general | solution.py:65
  135.1 10.0 %fusion.79 = (bf16[32,128,1,256]{3,2,1,0:T(2,128)(2,1)}, bf16[32,128,1,256]{3,2,1,0:T(2,128)(2,1)}) fusion(bf16[32,128,2,256]{3,2,1,0:T(2,128)(2,1)} %param.30), kind=kLoop, calls=%fused_computation.141 | loop fusion | bytes 8388608 | tf_op jit(solution)/shard_map/slice | solution.py:85
  145.1 9.7 %copy.108 = bf16[32,128,1,256]{1,3,0,2:T(8,128)(2,1)} copy(bf16[32,128,1,256]{3,2,1,0:T(2,128)(2,1)} %get-tuple-element.229) | data formatting | bytes 4194304
  154.9 8.7 %copy.109 = bf16[32,128,1,256]{1,3,0,2:T(8,128)(2,1)S(1)} copy(bf16[32,128,1,256]{3,2,1,0:T(2,128)(2,1)} %get-tuple-element.230) | data formatting | bytes 4194304
  163.6 2.2 fusion.56
  166.1 1.2 fusion.54
  167.3 24.2 %all-gather = f32[8192,4]{0,1:T(4,128)S(1)} all-gather(f32[512,4]{0,1:T(4,128)S(1)} %copy-done.13), channel_id=2, replica_groups=mesh['req'=16,'tp'=8] {'req'}, dimensions={0}, use_global_device_ids=true | all-gather | bytes 139264 | tf_op jit(solution)/shard_map/all_gather | solution.py:15
  191.5 23.1 %all-gather.1 = f32[8192,4]{0,1:T(4,128)S(1)} all-gather(f32[512,4]{0,1:T(4,128)S(1)} %copy-done.12), channel_id=3, replica_groups=mesh['req'=16,'tp'=8] {'req'}, dimensions={0}, use_global_device_ids=true | all-gather | bytes 139264 | tf_op jit(solution)/shard_map/all_gather | solution.py:15
  216.0 23.7 %while.19 = (s32[]{:T(128)}, f32[512,4]{0,1:T(4,128)S(1)}, f32[512,4]{0,1:T(4,128)S(1)}, f32[512,256]{0,1:T(8,128)S(1)}, f32[16,512,4]{1,2,0:T(4,128)S(1)}, /*in...) while((s32[]{:T(128)}, f32[512,4]{0,1:T(4,128)S(1)}, ...), condition=%wide.region_12.13_spmd, body=%wide.region_11.12_spmd.sunk | while | flops 405509 | bytes 3752087 | solution.py:21
  216.0 1.1 constant_dynamic-slice_fusion.3
  217.6 1.1 constant_dynamic-slice_fusion.3
  219.2 1.1 constant_dynamic-slice_fusion.3
  220.8 1.1 constant_dynamic-slice_fusion.3
  222.3 1.1 constant_dynamic-slice_fusion.3
  223.9 1.1 constant_dynamic-slice_fusion.3
  242.1 10.1 %copy.113 = bf16[256,8,2,1024]{3,1,2,0:T(8,128)(2,1)} copy(bf16[256,8,2,1024]{3,2,1,0:T(2,128)(2,1)} %bitcast.181) | data formatting | bytes 16777216
  252.3 12.5 %copy.94 = bf16[2048,2048]{1,0:T(8,128)(2,1)} copy(bf16[2048,2048]{0,1:T(8,128)(2,1)} %bitcast.180) | data formatting | bytes 16777216 | tf_op jit(solution)/shard_map/dot_general | solution.py:234
  264.8 37.0 %all-reduce.2.cloned.1.call-done = f32[32,2048]{1,0:T(8,128)} async-done(((f32[32,2048]{1,0:T(8,128)}), f32[32,2048]{1,0:T(8,128)}) %all-reduce.2.cloned.1.call-update) | async-done | bytes 262160 | tf_op jit(solution)/shard_map/psum | solution.py:230
  301.8 1.1 multiply_reduce_fusion
  302.9 6.1 %fusion.40 = f32[32,2,1024]{2,0,1:T(8,128)S(1)} fusion(bf16[2,1024,2048]{2,1,0:T(8,128)(2,1)} %bitcast.179, f32[32,2048]{1,0:T(8,128)S(1)} %get-tuple-element.219, f32[2048]{0:T(1024)S(1)} %convert_element_type.95, f32[32]{0:T(128)S(1)} %add_rsqrt_fusion.1), kind=kOutput, calls=%fused_computation.56 | convolution fusion | flops 268632064 | bytes 8921216 | tf_op jit(solution)/shard_map/dot_general | solution.py:234
  309.1 1.5 fusion.48
  310.6 29.8 %reduce-scatter.2.cloned.1.call-done = f32[32,256]{1,0:T(8,128)} async-done(((f32[32,2048]{1,0:T(8,128)}), f32[32,256]{1,0:T(8,128)}) %reduce-scatter.2.cloned.1.call-update) | async-done | bytes 32784 | tf_op jit(solution)/shard_map/reduce_scatter | solution.py:238
  340.5 1.4 add_convert_fusion.2
  (177 shorter events, 35.9 us)
Async XLA Ops:
  6.5 234.6 %copy-start = (bf16[256,2048]{1,0:T(8,128)(2,1)S(1)}, bf16[256,2048]{1,0:T(8,128)(2,1)}, u32[]{:S(2)}) copy-start(bf16[256,2048]{1,0:T(8,128)(2,1)} %param.25) | copy-start | bytes 3145732
  6.5 12.9 %copy-start.18 = (f32[32]{0:T(128)}, f32[32]{0:T(128)S(1)}, u32[]{:S(2)}) copy-start(f32[32]{0:T(128)S(1)} %multiply_exponential_fusion) | copy-start | bytes 388
  11.8 4.6 %copy-start.6 = (bf16[32,2048]{1,0:T(8,128)(2,1)S(1)}, bf16[32,2048]{1,0:T(8,128)(2,1)}, u32[]{:S(2)}) copy-start(bf16[32,2048]{1,0:T(8,128)(2,1)} %param.20) | copy-start | bytes 393220
  13.9 5.4 %copy-start.23 = (s32[8]{0:T(128)S(1)}, s32[8]{0:T(128)}, u32[]{:S(2)}) copy-start(s32[8]{0:T(128)} %param.33) | copy-start | bytes 100
  13.9 5.5 %copy-start.24 = (s32[16]{0:T(128)S(1)}, s32[16]{0:T(128)}, u32[]{:S(2)}) copy-start(s32[16]{0:T(128)} %param.34) | copy-start | bytes 196
  13.9 5.5 %copy-start.20 = (s32[32]{0:T(128)S(1)}, s32[32]{0:T(128)}, u32[]{:S(2)}) copy-start(s32[32]{0:T(128)} %param.35) | copy-start | bytes 388
  14.0 16.0 %copy-start.22 = (s32[16]{0:T(128)S(1)}, s32[16]{0:T(128)}, u32[]{:S(2)}) copy-start(s32[16]{0:T(128)} %param.36) | copy-start | bytes 196
  14.0 17.2 %copy-start.14 = (s32[512]{0:T(512)S(1)}, s32[512]{0:T(512)}, u32[]{:S(2)}) copy-start(s32[512]{0:T(512)} %param.37) | copy-start | bytes 6148
  16.4 17.0 %copy-start.3 = (bf16[8,256,2,256]{3,2,1,0:T(2,128)(2,1)S(1)}, bf16[8,256,2,256]{3,2,1,0:T(2,128)(2,1)}, u32[]{:S(2)}) copy-start(bf16[8,256,2,256]{3,2,1,0:T(2,128)(2,1)} %param.28) | copy-start | bytes 6291460
  19.3 0.7 copy-start.8
  21.6 33.0 %all-to-all-start = ((bf16[16,32,256]{2,1,0:T(8,128)(2,1)}), bf16[16,32,256]{2,1,0:T(8,128)(2,1)}, u32[]{:S(2)}, u32[]{:S(2)}) async-start(bf16[16,32,256]{2,1,0:T(8,128)(2,1)} %stack.11), calls=%async_computation | async-start | bytes 524288 | tf_op jit(solution)/shard_map/all_to_all | solution.py:167
  28.8 43.4 %all-gather.5.cloned.1.call-start = ((), (), s32[]{:S(2)}) async-start(), calls=%async_computation.2 | async-start | bytes 1179648 | tf_op jit(solution)/shard_map/all_gather | solution.py:150
  29.5 185.2 %all-gather.7.cloned.1.call-start = ((), (), s32[]{:S(2)}) async-start(), calls=%async_computation.3 | async-start | bytes 8912896 | tf_op jit(solution)/shard_map/all_gather | solution.py:15
  33.5 5.5 %copy-start.17 = (s32[1,256]{1,0:T(1,128)S(1)}, s32[1,256]{1,0:T(1,128)}, u32[]{:S(2)}) copy-start(s32[1,256]{1,0:T(1,128)} %param.32) | copy-start | bytes 3076
  42.1 12.3 %copy-start.19 = (f32[32]{0:T(128)S(1)}, f32[32]{0:T(128)}, u32[]{:S(2)}) copy-start(f32[32]{0:T(128)} %copy-done.18) | copy-start | bytes 388
  57.9 3.3 copy-start.4
  61.2 5.7 %copy-start.1 = (f32[4,512,2048]{2,1,0:T(8,128)}, f32[4,512,2048]{2,1,0:T(8,128)S(1)}, u32[]{:S(2)}) copy-start(f32[4,512,2048]{2,1,0:T(8,128)S(1)} %get-tuple-element.253) | copy-start | bytes 50331652
  61.2 10.9 %copy-start.9 = (f32[4,512]{1,0:T(4,128)}, f32[4,512]{1,0:T(4,128)S(1)}, u32[]{:S(2)}) copy-start(f32[4,512]{1,0:T(4,128)S(1)} %get-tuple-element.252) | copy-start | bytes 24580
  107.6 5.6 %copy-start.2 = (pred[512,2304]{1,0:T(8,128)(4,1)S(1)}, pred[512,2304]{1,0:T(8,128)(4,1)}, u32[]{:S(2)}) copy-start(pred[512,2304]{1,0:T(8,128)(4,1)} %pad_add_fusion) | copy-start | bytes 3538948
  113.3 5.1 %copy-start.10 = (f32[4,512]{1,0:T(4,128)S(1)}, f32[4,512]{1,0:T(4,128)}, u32[]{:S(2)}) copy-start(f32[4,512]{1,0:T(4,128)} %copy-done.9) | copy-start | bytes 24580
  113.3 5.1 %copy-start.11 = (f32[4,512]{1,0:T(4,128)S(1)}, f32[4,512]{1,0:T(4,128)}, u32[]{:S(2)}) copy-start(f32[4,512]{1,0:T(4,128)} %fusion.6) | copy-start | bytes 24580
  135.0 166.8 %all-reduce.2.cloned.1.call-start = ((), (), s32[]{:S(2)}) async-start(), calls=%async_computation.4 | async-start | bytes 524288 | tf_op jit(solution)/shard_map/psum | solution.py:230
  154.8 8.7 %copy-start.21 = (s32[32]{0:T(128)S(1)}, s32[32]{0:T(128)}, u32[]{:S(2)}) copy-start(s32[32]{0:T(128)} %param.35) | copy-start | bytes 388
  154.8 12.5 %copy-start.13 = (f32[512,4]{0,1:T(4,128)S(1)}, f32[512,4]{0,1:T(4,128)}, u32[]{:S(2)}) copy-start(f32[512,4]{0,1:T(4,128)} %get-tuple-element.245) | copy-start | bytes 24580
  154.9 36.7 %copy-start.12 = (f32[512,4]{0,1:T(4,128)S(1)}, f32[512,4]{0,1:T(4,128)}, u32[]{:S(2)}) copy-start(f32[512,4]{0,1:T(4,128)} %get-tuple-element.226) | copy-start | bytes 24580
  216.0 23.9 %copy-start.15 = (f32[32,4]{0,1:T(4,128)S(1)}, f32[32,4]{0,1:T(4,128)}, u32[]{:S(2)}) copy-start(f32[32,4]{0,1:T(4,128)} %get-tuple-element.224) | copy-start | bytes 1540
  242.1 98.4 %reduce-scatter.2.cloned.1.call-start = ((), (), s32[]{:S(2)}) async-start(), calls=%async_computation.5 | async-start | bytes 294912 | tf_op jit(solution)/shard_map/reduce_scatter | solution.py:238
  252.3 12.5 %copy-start.16 = (bf16[2048]{0:T(1024)(128)(2,1)S(1)}, bf16[2048]{0:T(1024)(128)(2,1)}, u32[]{:S(2)}) copy-start(bf16[2048]{0:T(1024)(128)(2,1)} %param.22) | copy-start | bytes 12292
  252.3 49.5 %copy-start.7 = (bf16[32,2048]{1,0:T(8,128)(2,1)S(1)}, bf16[32,2048]{1,0:T(8,128)(2,1)}, u32[]{:S(2)}) copy-start(bf16[32,2048]{1,0:T(8,128)(2,1)} %param.20) | copy-start | bytes 393220
  302.9 6.2 %copy-start.5 = (bf16[1024,2048]{1,0:T(8,128)(2,1)S(1)}, bf16[1024,2048]{1,0:T(8,128)(2,1)}, u32[]{:S(2)}) copy-start(bf16[1024,2048]{1,0:T(8,128)(2,1)} %param.27) | copy-start | bytes 12582916
Sparse Core Ops, SparseCore 0:
  31.3 26.0 all-gather.4
  135.2 74.2 all-gather.6
  242.2 59.5 all-reduce.1
  310.7 29.6 reduce-scatter.1
